TPU v7x, 32 devices: a whole 2x2x4 slice. The times are simulated.
32 devices in a mesh: grp: 2 (over y), samp: 4 (over z), snp: 4 (over x, core).
Axes of the slice: x: 2, y: 2, z: 4, core: 2. Of those that a mesh axis runs over, the one named last changes fastest.
Arguments:
- genotypes: int32 [2048, 8192], P(('grp', 'samp'), 'snp'), parts along dimension 0, may hold values from 0 to 2730, as said below
- basis_cols: bfloat16 [16384, 256], P(('grp', 'snp')), parts along dimension 0, may hold values from -0.0625 to 0.0625
Outputs:
- y_block: float32 [8, 4, 512, 256], P(('grp', 'snp'), 'samp'), parts along dimension 0
- r_factor: float32 [512, 256], P('grp'), parts along dimension 0
- q_next: float32 [8, 4, 512, 256], P(('grp', 'snp'), 'samp'), parts along dimension 0
There are 2 independent parts, one for each index of `grp`. A program takes and returns all parts, laid end to end along the dimension named above; each array names one. Nothing has to cross between parts.
Inputs may be any that keep to these rules, and one draw needn't show every extreme that they name: `genotypes`: each word packs 6 dosages of 0, 1 or 2 in pairs of bits: bits 2 t and 2 t + 1 of word (w, p) hold the dosage of sample 6 w + t at SNP p, t from 0 to 5; bits 12 and up are zero.
All inputs are finite; a program needn't handle non-finite values.
Results may differ from a plain program's by a relative error of at most 0.0025.
Values may be sent and summed in bfloat16 or wider, within the bound.
A program may use at most 64 MiB of HBM per device.

v0:
```python
import jax
import jax.numpy as jnp
from jax import lax
from jax.sharding import PartitionSpec as P


def unpack_counts(genotypes):
    planes = [
        jnp.bitwise_and(jnp.right_shift(genotypes, 2 * shift_pos), 3) for shift_pos in range(6)
    ]
    local_counts = planes[0].sum(axis=0)
    for plane_item in planes[1:]:
        local_counts = local_counts + plane_item.sum(axis=0)
    dosage = jnp.stack([plane_item.astype(jnp.bfloat16) for plane_item in planes], axis=1)
    dosage = dosage.reshape(genotypes.shape[0] * 6, genotypes.shape[1])
    return (dosage, local_counts)


def per_device(genotypes, basis_cols):
    dosage, local_counts = unpack_counts(genotypes)
    sample_rows, snp_cols = dosage.shape
    width = basis_cols.shape[1]
    totals = lax.psum(local_counts, "samp")
    samples = sample_rows * lax.axis_size("samp")
    allele_mean = totals.astype(jnp.float32) / jnp.float32(samples)
    center = jnp.dot(allele_mean, basis_cols.astype(jnp.float32), precision=lax.Precision.HIGHEST)
    inv_root = jnp.float32(1.0) / jnp.sqrt(jnp.float32(samples))
    contract_rows = (((0,), (0,)), ((), ()))
    product_term = jnp.dot(dosage, basis_cols, preferred_element_type=jnp.float32) - center[None, :]
    score_rows = lax.psum(product_term, "snp").astype(jnp.bfloat16)
    y_local = lax.psum_scatter(
        lax.dot_general(dosage, score_rows, contract_rows, preferred_element_type=jnp.float32)
        * inv_root,
        "samp",
        scatter_dimension=0,
        tiled=True,
    )
    snp_total = snp_cols * lax.axis_size("snp")
    local_gram = jnp.dot(y_local.T, y_local, precision=lax.Precision.HIGHEST) / jnp.float32(
        snp_total
    )
    gram_sum = lax.psum(local_gram, ("samp", "snp"))
    lower_factor = jnp.linalg.cholesky(gram_sum)
    q_next = lax.linalg.triangular_solve(
        lower_factor, y_local, left_side=False, lower=True, transpose_a=True
    )
    layout = (1, 1, y_local.shape[0], width)
    return (y_local.reshape(layout), lower_factor.T, q_next.reshape(layout))


def solution(mesh):
    return jax.shard_map(
        per_device,
        mesh=mesh,
        in_specs=(P(("grp", "samp"), "snp"), P(("grp", "snp"), None)),
        out_specs=(
            P(("grp", "snp"), "samp", None, None),
            P("grp", None),
            P(("grp", "snp"), "samp", None, None),
        ),
        check_vma=False,
    )
```

profile of v0, /device:TPU:0, one launch (start us, length us, event | category | flops | bytes accessed | tf_op | source)
XLA Modules:
  0.0 291.1 jit_solution(1570081549035918999)
XLA Ops:
  7.2 0.0 copy-start
  7.2 0.0 copy-start.1
  7.2 0.0 reduce-scatter.2.cloned.1.call-start
  7.2 2.0 fusion.23
  9.2 0.3 copy-done.1
  9.5 1.2 fusion.2
  10.7 0.3 fusion.21
  11.0 0.3 fusion.19
  11.3 0.3 fusion.17
  11.5 0.3 fusion.15
  11.8 0.3 fusion.13
  12.1 6.9 %copy.9 = bf16[256,6,2048]{2,1,0:T(8,128)(2,1)} copy(bf16[256,6,2048]{2,0,1:T(8,128)(2,1)S(1)} %fusion.13) | data formatting | bytes 12582912 | tf_op jit(solution)/shard_map/stack | solution.py:14
  18.9 11.1 %reshape.33 = bf16[1536,2048]{1,0:T(8,128)(2,1)} reshape(bf16[256,6,2048]{2,1,0:T(8,128)(2,1)} %copy.9) | data formatting | bytes 12582912 | tf_op jit(solution)/shard_map/reshape | solution.py:15
  30.0 10.0 %psum.21 = s32[2048]{0:T(1024)S(1)} all-reduce(s32[2048]{0:T(1024)S(1)} %add_add_fusion), channel_id=1, replica_groups=mesh['grp'=2,'samp'=4,'snp'=4] {'samp'}, use_global_device_ids=true, to_apply=%region_6.0 | all-reduce | flops 2048 | bytes 16384 | tf_op jit(solution)/shard_map/psum | solution.py:23
  40.1 0.0 copy-done
  40.1 0.5 fusion.36
  40.6 4.6 %convolution_subtract_fusion = f32[1536,256]{1,0:T(8,128)S(1)} fusion(bf16[1536,2048]{1,0:T(8,128)(2,1)} %reshape.33, bf16[2048,256]{1,0:T(8,128)(2,1)S(1)} %copy-done, f32[256]{0:T(256)S(1)} %bitcast.72), kind=kOutput, calls=%fused_computation.3 | convolution fusion | flops 1611005952 | bytes 8913920 | tf_op jit(solution)/shard_map/dot_general | solution.py:29
  45.2 32.6 %all-reduce.5 = bf16[1536,256]{1,0:T(8,128)(2,1)S(1)} all-reduce(f32[1536,256]{1,0:T(8,128)S(1)} %convolution_subtract_fusion), channel_id=1, replica_groups=mesh['grp'=2,'samp'=4,'snp'=4] {'snp'}, use_global_device_ids=true, to_apply=%region_7.0 | all-reduce | flops 393216 | bytes 2359296 | tf_op jit(solution)/shard_map/psum | solution.py:30
  77.8 6.0 %convolution_multiply_fusion = f32[2048,256]{1,0:T(8,128)} fusion(bf16[1536,2048]{1,0:T(8,128)(2,1)} %reshape.33, bf16[1536,256]{1,0:T(8,128)(2,1)S(1)} %all-reduce.5), kind=kOutput, calls=%fused_computation.2 | convolution fusion | flops 1611137024 | bytes 9175040 | tf_op jit(solution)/shard_map/dot_general | solution.py:32
  83.8 0.0 reduce-scatter.2.cloned.1.call-update
  83.9 0.0 all-reduce.4.cloned.1.call-start
  83.9 42.3 %reduce-scatter.2.cloned.1.call-done = f32[512,256]{1,0:T(8,128)} async-done(((f32[2048,256]{1,0:T(8,128)}), f32[512,256]{1,0:T(8,128)}) %reduce-scatter.2.cloned.1.call-update) | async-done | bytes 524304 | tf_op jit(solution)/shard_map/reduce_scatter | solution.py:31
  126.2 2.9 convolution_multiply_fusion.1
  129.1 0.0 all-reduce.4.cloned.1.call-update
  129.2 90.0 %all-reduce.4.cloned.1.call-done = f32[256,256]{0,1:T(8,128)} async-done(((f32[256,256]{0,1:T(8,128)}), f32[256,256]{0,1:T(8,128)}) %all-reduce.4.cloned.1.call-update) | async-done | bytes 262160 | tf_op jit(solution)/shard_map/psum | solution.py:42
  219.2 1.1 copy.11
  220.2 0.0 copy-start.2
  220.3 1.0 fusion.27
  221.3 11.7 %cholesky.50 = f32[128,128]{1,0:T(8,128)S(1)} custom-call(f32[128,128]{1,0:T(8,128)S(1)} %cholesky.118), custom_call_target="Cholesky" | custom-call | tf_op jit(solution)/shard_map/jit(cholesky)/cholesky | solution.py:43
  233.1 9.8 %custom-call.14 = f32[1,128,128]{1,2,0:T(8,128)S(1)} custom-call(f32[1,128,128]{2,1,0:T(8,128)S(1)} %get-tuple-element.38), custom_call_target="InvertDiagBlocksLowerTriangular" | custom-call | tf_op jit(solution)/shard_map/jit(cholesky)/cholesky | solution.py:43
  242.9 0.2 constant_dynamic-update-slice_fusion.1
  243.1 0.3 convolution_subtract_fusion.2
  243.4 11.7 %cholesky.105 = f32[128,128]{1,0:T(8,128)S(1)} custom-call(f32[128,128]{1,0:T(8,128)S(1)} %convolution_subtract_fusion.2), custom_call_target="Cholesky" | custom-call | tf_op jit(solution)/shard_map/jit(cholesky)/cholesky | solution.py:43
  255.1 0.6 compare_reduce_fusion
  257.1 0.8 copy.12
  258.0 0.1 triangular_solve.43
  258.0 4.1 %while.1 = (s32[]{:T(128)}, f32[256,256]{1,0:T(8,128)S(1)}, s32[2,2]{1,0:T(2,128)S(1)}, f32[2,128,128]{2,1,0:T(8,128)S(1)}, s32[]{:T(128)}) while((s32[]{:T(128)}, f32[256,256]{1,0:T(8,128)S(1)}, s32[2,2]{1,0:T(2,128)S(1)}, f32[2,128,128]{2,1,0:T(8,128)S(1)}, s32[]{:T(128)}) %tuple.35), condition=%wide.while_cond, body=%wide.while_body.sunk | while | flops 2 | bytes 131189 | solution.py:44
  258.0 0.6 fusion.50
  258.6 1.4 bitcast_dynamic-update-slice_fusion.2
  260.1 0.6 fusion.50
  260.7 1.4 bitcast_dynamic-update-slice_fusion.2
  262.1 19.7 %custom-call.15 = f32[2,128,128]{1,2,0:T(8,128)S(1)} custom-call(f32[2,128,128]{2,1,0:T(8,128)S(1)} %get-tuple-element.10), custom_call_target="InvertDiagBlocksLowerTriangular" | custom-call | tf_op jit(solution)/shard_map/triangular_solve | solution.py:44
  281.8 0.0 copy-done.2
  281.8 0.4 fusion.25
  282.2 0.6 convolution_subtract_fusion.1
  282.8 0.4 fusion.30
  283.3 1.0 copy.13
  (12 shorter events, 0.2 us)
Async XLA Ops:
  7.2 32.9 %copy-start = (bf16[2048,256]{1,0:T(8,128)(2,1)S(1)}, bf16[2048,256]{1,0:T(8,128)(2,1)}, u32[]{:S(2)}) copy-start(bf16[2048,256]{1,0:T(8,128)(2,1)} %param.3) | copy-start | bytes 3145732
  7.2 2.3 copy-start.1
  7.2 119.0 %reduce-scatter.2.cloned.1.call-start = ((), (), s32[]{:S(2)}) async-start(), calls=%async_computation.1 | async-start | bytes 2621440 | tf_op jit(solution)/shard_map/reduce_scatter | solution.py:31
  83.9 135.3 %all-reduce.4.cloned.1.call-start = ((), (), s32[]{:S(2)}) async-start(), calls=%async_computation.2 | async-start | bytes 524288 | tf_op jit(solution)/shard_map/psum | solution.py:42
  220.2 61.6 %copy-start.2 = (f32[512,256]{1,0:T(8,128)S(1)}, f32[512,256]{1,0:T(8,128)}, u32[]{:S(2)}) copy-start(f32[512,256]{1,0:T(8,128)} %reduce-scatter.2.cloned.1.call-done) | copy-start | bytes 1572868
Sparse Core Ops, SparseCore 0:
  84.0 42.1 reduce-scatter.1
  130.2 88.9 all-reduce.3
where the time goes:
time: 292 us; the launch traced here: 291 us
  waiting for transfers between devices  132 us (45%)
  other arithmetic  59.3 us (20%)
  blocking collectives  42.7 us (15%)
  local copies, waits for them, and re-layouts  25.3 us (9%)
  matrix products  15.9 us (5%)
  between operations  15.6 us (5%)
    psum x1, waiting for transfers between devices, per_device(): gram_sum = lax.psum(local_gram, ('samp', 'snp'))  90 us
    reduce_scatter x1, waiting for transfers between devices, per_device(): lax.psum_scatter(lax.dot_general(dosage, score_rows, contract_rows, prefe...  42.3 us
    another operation x6, other arithmetic, per_device(): lower_factor = jnp.linalg.cholesky(gram_sum)  33.9 us
    psum x1, blocking collectives, per_device(): score_rows = lax.psum(product_term, 'snp').astype(jnp.bfloat16)  32.6 us
    another operation x3, other arithmetic, per_device(): lax.linalg.triangular_solve(lower_factor, y_local, left_side=False, lower...  19.7 us
    reshape x1, local copies, waits for them, and re-layouts, unpack_counts(): dosage = dosage.reshape(genotypes.shape[0] * 6, genotypes.shape[1])  11.1 us
    psum x1, blocking collectives, per_device(): totals = lax.psum(local_counts, 'samp')  10 us
    another operation x1, local copies, waits for them, and re-layouts, unpack_counts(): jnp.stack([plane_item.astype(jnp.bfloat16) for plane_item in planes], axi...  6.86 us
  transfers between devices with their start and end apart: 2, of which 2 were waited for; matrix products, arithmetic and copies ran while one was open for 0% of the time, Pallas kernels for 0%

commit v1 on v0

v1 whole, which is shorter than its diff:
```python
import functools
import jax
import jax.numpy as jnp
from jax import lax
from jax.experimental import pallas as pl
from jax.experimental.pallas import tpu as pltpu
from jax.sharding import PartitionSpec as P

PLANES = 6
MESH = pl.DeviceIdType.MESH
F32 = jnp.float32
BF16 = jnp.bfloat16
HIGH = lax.Precision.HIGHEST
LEVELS = 32767.0


def log2(n):
    bits = n.bit_length() - 1
    assert 1 << bits == n
    return bits


def segments(me, bits, rows):
    base, steps = 0, []
    for b in range(bits):
        bit = (me // (1 << b)) % 2
        half = rows >> (b + 1)
        steps.append((base + bit * half, base + (1 - bit) * half, half))
        base = base + bit * half
    return steps


def main_kernel(
    n_snp, n_samp, chunks,
    g_ref, b_ref, y_ref, gram_ref,
    part, rs_rx, scores, dose_t, cs_tx, cs_rx, ct_tx, ct_rx,
    yq, ysc, yq_rx, ysc_rx, gwork, g_rx, gs_rx, gout,
    rs_s, rs_r, ag_s, ag_r, cs_s, cs_r, ct_s, ct_r, yq_s, yq_r, ysc_s, ysc_r,
    gr_s, gr_r, gs_s, gs_r, ga_s, ga_r,
):
    snp, samp = lax.axis_index("snp"), lax.axis_index("samp")
    bits = log2(n_snp)
    words = g_ref.shape[0]
    rows = PLANES * words
    width = b_ref.shape[1]
    crow = rows // chunks
    samples = rows * n_samp

    def copy(src, dst, ssem, rsem, axis, peer):
        return pltpu.make_async_remote_copy(
            src_ref=src, dst_ref=dst, send_sem=ssem, recv_sem=rsem,
            device_id={axis: peer}, device_id_type=MESH,
        )

    def partner(b):
        bit = (snp // (1 << b)) % 2
        return snp + (1 - 2 * bit) * (1 << b)

    barrier = pltpu.get_barrier_semaphore()
    for d in range(1, n_snp):
        pl.semaphore_signal(barrier, inc=1, device_id={"snp": lax.rem(snp + d, n_snp)}, device_id_type=MESH)
    for d in range(1, n_samp):
        pl.semaphore_signal(barrier, inc=1, device_id={"samp": lax.rem(samp + d, n_samp)}, device_id_type=MESH)

    steps = segments(snp, bits, crow)

    def rows_at(c, off, size):
        return pl.ds(pl.multiple_of(c * crow + off, 16), size)

    def rs_copy(c, b):
        keep, send, half = steps[b]
        return copy(
            part.at[rows_at(c, send, half)],
            rs_rx.at[pl.ds(c * crow + crow - 2 * half, half)],
            rs_s.at[c, b], rs_r.at[c, b], "snp", partner(b),
        )

    def ag_copy(c, b):
        keep, send, half = steps[b]
        seg = rows_at(c, keep, half)
        return copy(scores.at[seg], scores.at[seg], ag_s.at[c, b], ag_r.at[c, b], "snp", partner(b))

    per = PLANES // chunks
    colsum = jnp.zeros((8, width), F32)
    for c in range(chunks):
        for t in range(c * per, (c + 1) * per):
            dose = ((g_ref[...] >> (2 * t)) & 3).astype(F32).astype(BF16)
            prod = jnp.dot(dose, b_ref[...], preferred_element_type=F32)
            part[pl.ds(t * words, words), :] = prod
            colsum = colsum + prod.reshape(words // 8, 8, width).sum(axis=0)
        if c == 0:
            pl.semaphore_wait(barrier, n_snp + n_samp - 2)
        rs_copy(c, 0).start()
    cs_tx[...] = colsum

    def cs_copy(d):
        return copy(cs_tx, cs_rx.at[d], cs_s.at[d], cs_r.at[d], "snp", lax.rem(snp + d, n_snp))

    def ct_copy(d):
        return copy(ct_tx, ct_rx.at[d], ct_s.at[d], ct_r.at[d], "samp", lax.rem(samp + d, n_samp))

    for d in range(1, n_snp):
        cs_copy(d).start()

    def reduce_step(b, center=None):
        for c in range(chunks):
            keep, send, half = steps[b]
            rs_copy(c, b).wait()
            seg = rows_at(c, keep, half)
            total = part[seg, :] + rs_rx[pl.ds(c * crow + crow - 2 * half, half), :]
            if b + 1 < bits:
                part[seg, :] = total
                rs_copy(c, b + 1).start()
            else:
                scores[seg, :] = (total - center).astype(BF16)
                ag_copy(c, b).start()

    for b in range(bits - 1):
        reduce_step(b)
        if b == 0:
            tot = colsum
            for d in range(1, n_snp):
                cs_copy(d).wait()
                tot = tot + cs_rx[d]
            ct_tx[...] = tot
            for d in range(1, n_samp):
                ct_copy(d).start()
    word_t = g_ref[...].T
    for t in range(PLANES):
        dose_t[:, t * words:(t + 1) * words] = ((word_t >> (2 * t)) & 3).astype(F32).astype(BF16)
    for d in range(1, n_samp):
        ct_copy(d).wait()
        tot = tot + ct_rx[d]
    center = tot.sum(axis=0, keepdims=True) / F32(samples)
    reduce_step(bits - 1, center)
    for b in range(bits - 1, -1, -1):
        for c in range(chunks):
            ag_copy(c, b).wait()
            if b:
                ag_copy(c, b - 1).start()

    inv_root = F32(1.0) / jnp.sqrt(F32(samples))
    own_rows = y_ref.shape[0]

    def y_part(owner):
        blk = dose_t[pl.ds(pl.multiple_of(owner * own_rows, 16), own_rows), :]
        return jnp.dot(blk, scores[...], preferred_element_type=F32) * inv_root

    def y_copies(d):
        to = lax.rem(samp + d, n_samp)
        return (
            copy(yq.at[d], yq_rx.at[d], yq_s.at[d], yq_r.at[d], "samp", to),
            copy(ysc.at[d], ysc_rx.at[d], ysc_s.at[d], ysc_r.at[d], "samp", to),
        )

    for d in range(1, n_samp):
        block = y_part(lax.rem(samp + d, n_samp))
        top = jnp.maximum(jnp.max(jnp.abs(block), axis=0, keepdims=True), F32(1e-30))
        yq[d] = jnp.round(block * (F32(LEVELS) / top)).astype(jnp.int32).astype(jnp.int16)
        ysc[d] = jnp.broadcast_to(top * F32(1.0 / LEVELS), (8, width))
        for cp in y_copies(d):
            cp.start()
    y = y_part(samp)
    for d in range(1, n_samp):
        for cp in y_copies(d):
            cp.wait()
        y = y + yq_rx[d].astype(jnp.int32).astype(F32) * ysc_rx[d][0:1, :]
    y_ref[...] = y

    snp_total = dose_t.shape[0] * n_snp
    gwork[...] = lax.dot_general(y, y, (((0,), (0,)), ((), ())), precision=HIGH, preferred_element_type=F32) / F32(snp_total)
    gsteps = segments(snp, bits, width)

    def at(off, size):
        return pl.ds(pl.multiple_of(off, 8), size)

    def gr_copy(b):
        keep, send, half = gsteps[b]
        return copy(gwork.at[at(send, half)], g_rx.at[pl.ds(width - 2 * half, half)], gr_s.at[b], gr_r.at[b], "snp", partner(b))

    def ga_copy(b):
        keep, send, half = gsteps[b]
        return copy(gout.at[at(keep, half)], gout.at[at(keep, half)], ga_s.at[b], ga_r.at[b], "snp", partner(b))

    for b in range(bits):
        keep, send, half = gsteps[b]
        gr_copy(b).start()
        gr_copy(b).wait()
        mine = gwork[at(keep, half), :] + g_rx[pl.ds(width - 2 * half, half), :]
        gwork[at(keep, half), :] = mine
    keep, send, half = gsteps[bits - 1]

    def gs_copy(d):
        return copy(gwork.at[at(keep, half)], gs_rx.at[samp], gs_s.at[d], gs_r.at[d], "samp", lax.rem(samp + d, n_samp))

    for d in range(1, n_samp):
        gs_copy(d).start()
    gs_rx[samp] = mine
    for d in range(1, n_samp):
        gs_copy(d).wait()
    total = gs_rx[0]
    for j in range(1, n_samp):
        total = total + gs_rx[j]
    gout[at(keep, half), :] = total
    for b in range(bits - 1, -1, -1):
        ga_copy(b).start()
        ga_copy(b).wait()
    gram_ref[...] = gout[...]


def eliminate(a):
    n = a.shape[0]
    groups = n // 8
    lane = lax.broadcasted_iota(jnp.int32, (8, n), 1)
    sub = lax.broadcasted_iota(jnp.int32, (8, n), 0)
    left = [a[8 * g:8 * g + 8, :] for g in range(groups)]
    right = [jnp.where(lane == sub + 8 * g, F32(1.0), F32(0.0)) for g in range(groups)]
    for j in range(n):
        g0, s = j // 8, j % 8
        row = left[g0][s:s + 1, :]
        inv = F32(1.0) / row[:, j:j + 1]
        row_l = row * inv
        row_r = right[g0][s:s + 1, :] * inv
        for g in range(g0, groups):
            if g == g0 and s == 7:
                continue
            col = jnp.broadcast_to(left[g][:, j:j + 1], (8, n))
            if g == g0:
                col = jnp.where(sub > s, col, F32(0.0))
            left[g] = left[g] - col * row_l
            right[g] = right[g] - col * row_r
    ups, invs = [], []
    for g in range(groups):
        diag = jnp.sum(jnp.where(lane == sub + 8 * g, left[g], F32(0.0)), axis=1, keepdims=True)
        scale = F32(1.0) / jnp.sqrt(diag)
        ups.append(jnp.where(lane >= sub + 8 * g, left[g] * scale, F32(0.0)))
        invs.append(right[g] * scale)
    return jnp.concatenate(ups, axis=0), jnp.concatenate(invs, axis=0)


def factor_kernel(gram_ref, y_ref, r_ref, q_ref, inv_ref):
    width = gram_ref.shape[0]
    nb = min(128, width)
    blocks = width // nb

    def blk(ref, i, j):
        return ref[i * nb:(i + 1) * nb, j * nb:(j + 1) * nb]

    def dot(a, b, dims):
        return lax.dot_general(a, b, (dims, ((), ())), precision=HIGH, preferred_element_type=F32)

    r_ref[...] = jnp.zeros_like(r_ref)
    inv_ref[...] = jnp.zeros_like(inv_ref)
    for k in range(blocks):
        a = blk(gram_ref, k, k)
        for m in range(k):
            a = a - dot(blk(r_ref, m, k), blk(r_ref, m, k), ((0,), (0,)))
        upper, inv = eliminate(a)
        r_ref[k * nb:(k + 1) * nb, k * nb:(k + 1) * nb] = upper
        inv_ref[k * nb:(k + 1) * nb, k * nb:(k + 1) * nb] = inv
        for j in range(k + 1, blocks):
            a = blk(gram_ref, k, j)
            for m in range(k):
                a = a - dot(blk(r_ref, m, k), blk(r_ref, m, j), ((0,), (0,)))
            r_ref[k * nb:(k + 1) * nb, j * nb:(j + 1) * nb] = dot(inv, a, ((1,), (0,)))
        for j in range(k):
            acc = jnp.zeros((nb, nb), F32)
            for m in range(j, k):
                acc = acc + dot(blk(r_ref, m, k), blk(inv_ref, m, j), ((0,), (0,)))
            inv_ref[k * nb:(k + 1) * nb, j * nb:(j + 1) * nb] = -dot(inv, acc, ((1,), (0,)))
    q_ref[...] = dot(y_ref[...], inv_ref[...], ((1,), (1,)))


def per_device(n_snp, n_samp, genotypes, basis_cols):
    words, snps = genotypes.shape
    width = basis_cols.shape[1]
    rows = PLANES * words
    chunks = 3
    own = snps // n_samp
    bits = log2(n_snp)
    vmem = pl.BlockSpec(memory_space=pltpu.VMEM)
    dma = pltpu.SemaphoreType.DMA
    y, gram = pl.pallas_call(
        functools.partial(main_kernel, n_snp, n_samp, chunks),
        out_shape=(
            jax.ShapeDtypeStruct((own, width), F32),
            jax.ShapeDtypeStruct((width, width), F32),
        ),
        in_specs=[vmem, vmem],
        out_specs=(vmem, vmem),
        scratch_shapes=[
            pltpu.VMEM((rows, width), F32),
            pltpu.VMEM((rows, width), F32),
            pltpu.VMEM((rows, width), BF16),
            pltpu.VMEM((snps, rows), BF16),
            pltpu.VMEM((8, width), F32),
            pltpu.VMEM((n_snp, 8, width), F32),
            pltpu.VMEM((8, width), F32),
            pltpu.VMEM((n_samp, 8, width), F32),
            pltpu.VMEM((n_samp, own, width), jnp.int16),
            pltpu.VMEM((n_samp, 8, width), F32),
            pltpu.VMEM((n_samp, own, width), jnp.int16),
            pltpu.VMEM((n_samp, 8, width), F32),
            pltpu.VMEM((width, width), F32),
            pltpu.VMEM((width, width), F32),
            pltpu.VMEM((n_samp, width // n_snp, width), F32),
            pltpu.VMEM((width, width), F32),
            dma((chunks, bits)), dma((chunks, bits)), dma((chunks, bits)), dma((chunks, bits)),
            dma((n_snp,)), dma((n_snp,)), dma((n_samp,)), dma((n_samp,)),
            dma((n_samp,)), dma((n_samp,)), dma((n_samp,)), dma((n_samp,)),
            dma((bits,)), dma((bits,)), dma((n_samp,)), dma((n_samp,)), dma((bits,)), dma((bits,)),
        ],
        compiler_params=pltpu.CompilerParams(collective_id=0, has_side_effects=True),
    )(genotypes, basis_cols)
    r_factor, q_next = pl.pallas_call(
        factor_kernel,
        out_shape=(
            jax.ShapeDtypeStruct((width, width), F32),
            jax.ShapeDtypeStruct((own, width), F32),
        ),
        in_specs=[vmem, vmem],
        out_specs=(vmem, vmem),
        scratch_shapes=[pltpu.VMEM((width, width), F32)],
    )(gram, y)
    layout = (1, 1, own, width)
    return (y.reshape(layout), r_factor, q_next.reshape(layout))


def solution(mesh):
    return jax.shard_map(
        functools.partial(per_device, mesh.shape["snp"], mesh.shape["samp"]),
        mesh=mesh,
        in_specs=(P(("grp", "samp"), "snp"), P(("grp", "snp"), None)),
        out_specs=(
            P(("grp", "snp"), "samp", None, None),
            P("grp", None),
            P(("grp", "snp"), "samp", None, None),
        ),
        check_vma=False,
    )
```

time: 292 us -> 94.7 us (0.32)
  waiting for transfers between devices: 132 us -> 0 us
  Pallas kernels: 0 us -> 92 us
  other arithmetic: 59.3 us -> 0 us
  blocking collectives: 42.7 us -> 0 us
  local copies, waits for them, and re-layouts: 25.3 us -> 1.87 us
  matrix products: 15.9 us -> 0 us
  between operations: 15.6 us -> 0.64 us
    pallas_call x0 -> x2, Pallas kernels: none -> 92 us  [the longest x1 67.2 us: per_device(): pl.pallas_call(functools.partial(main_kernel, n_snp, n_samp, chunks), out...]
    psum x1 -> x0, waiting for transfers between devices: 90 us -> none  [per_device(): gram_sum = lax.psum(local_gram, ('samp', 'snp'))]
    another operation x10 -> x0, other arithmetic: 53.9 us -> none  [the longest x6 33.9 us: per_device(): lower_factor = jnp.linalg.cholesky(gram_sum)]
    psum x2 -> x0, blocking collectives: 42.7 us -> none  [the longest x1 32.6 us: per_device(): score_rows = lax.psum(product_term, 'snp').astype(jnp.bfloat16)]
    reduce_scatter x1 -> x0, waiting for transfers between devices: 42.3 us -> none  [per_device(): lax.psum_scatter(lax.dot_general(dosage, score_rows, contract_rows, prefe...]
    dot_general x4 -> x0, matrix products: 14.1 us -> none  [the longest x1 6.05 us: per_device(): lax.dot_general(dosage, score_rows, contract_rows, preferred_element_type...]
    reshape x1 -> x0, local copies, waits for them, and re-layouts: 11.1 us -> none  [unpack_counts(): dosage = dosage.reshape(genotypes.shape[0] * 6, genotypes.shape[1])]
    another operation x10 -> x0, local copies, waits for them, and re-layouts: 11 us -> none  [the longest x1 6.86 us: unpack_counts(): jnp.stack([plane_item.astype(jnp.bfloat16) for plane_item in planes], axi...]
  transfers between devices with their start and end apart: 2 -> 0, of which waited for: 2 -> 0; matrix products, arithmetic and copies ran while one was open for 0% -> 0% of each run, Pallas kernels for 0% -> 0%
where the time goes in v1:
time: 94.7 us; the launch traced here: 94.5 us
  Pallas kernels  92 us (97%)
  local copies, waits for them, and re-layouts  1.87 us (2%)
    pallas_call x1, Pallas kernels, per_device(): pl.pallas_call(functools.partial(main_kernel, n_snp, n_samp, chunks), out...  67.2 us
    pallas_call x1, Pallas kernels, per_device(): pl.pallas_call(factor_kernel, out_shape=(jax.ShapeDtypeStruct((width, wid...  24.8 us

profile of v1, /device:TPU:0, one launch (start us, length us, event | category | flops | bytes accessed | tf_op | source)
XLA Modules:
  0.0 94.5 jit_solution(11786516075965632564)
XLA Ops:
  0.6 67.2 %shard_map.49 = (f32[512,256]{1,0:T(8,128)}, f32[256,256]{1,0:T(8,128)}) custom-call(s32[256,2048]{1,0:T(8,128)} %g_ref.1, bf16[2048,256]{1,0:T(8,128)(2,1)} %b_ref.1), custom_call_target="tpu_custom_call" | custom-call | tf_op jit(solution)/shard_map/pallas_call | solution.py:283
  67.8 24.8 %shard_map.50 = (f32[256,256]{1,0:T(8,128)}, f32[512,256]{1,0:T(8,128)}) custom-call(f32[256,256]{1,0:T(8,128)} %get-tuple-element.8.gram_ref, f32[512,256]{1,0:T(8,128)} %get-tuple-element.7.y_ref), custom_call_target="tpu_custom_call" | custom-call | tf_op jit(solution)/shard_map/pallas_call | solution.py:315
  92.6 1.9 %copy.6 = f32[1,1,512,256]{3,2,1,0:T(8,128)} copy(f32[1,1,512,256]{3,2,1,0:T(8,128)} %bitcast.2) | data formatting | bytes 1048576

commit v2 on v1

--- a/solution.py
+++ b/solution.py
@@ -168,15 +168,21 @@
     y_ref[...] = y
 
     snp_total = dose_t.shape[0] * n_snp
-    gwork[...] = lax.dot_general(y, y, (((0,), (0,)), ((), ())), precision=HIGH, preferred_element_type=F32) / F32(snp_total)
-    gsteps = segments(snp, bits, width)
+    half_w = width // 2
+    packed = width - width // 4
+    top = lax.dot_general(y[:, :half_w], y, (((0,), (0,)), ((), ())), precision=HIGH, preferred_element_type=F32)
+    low = lax.dot_general(y[:, half_w:], y[:, half_w:], (((0,), (0,)), ((), ())), precision=HIGH, preferred_element_type=F32)
+    gwork[:half_w, :] = top / F32(snp_total)
+    gwork[half_w:, :half_w] = low[:half_w // 2, :] / F32(snp_total)
+    gwork[half_w:, half_w:] = low[half_w // 2:, :] / F32(snp_total)
+    gsteps = segments(snp, bits, packed)
 
     def at(off, size):
         return pl.ds(pl.multiple_of(off, 8), size)
 
     def gr_copy(b):
         keep, send, half = gsteps[b]
-        return copy(gwork.at[at(send, half)], g_rx.at[pl.ds(width - 2 * half, half)], gr_s.at[b], gr_r.at[b], "snp", partner(b))
+        return copy(gwork.at[at(send, half)], g_rx.at[pl.ds(packed - 2 * half, half)], gr_s.at[b], gr_r.at[b], "snp", partner(b))
 
     def ga_copy(b):
         keep, send, half = gsteps[b]
@@ -186,7 +192,7 @@
         keep, send, half = gsteps[b]
         gr_copy(b).start()
         gr_copy(b).wait()
-        mine = gwork[at(keep, half), :] + g_rx[pl.ds(width - 2 * half, half), :]
+        mine = gwork[at(keep, half), :] + g_rx[pl.ds(packed - 2 * half, half), :]
         gwork[at(keep, half), :] = mine
     keep, send, half = gsteps[bits - 1]
 
@@ -205,7 +211,10 @@
     for b in range(bits - 1, -1, -1):
         ga_copy(b).start()
         ga_copy(b).wait()
-    gram_ref[...] = gout[...]
+    gram_ref[:half_w, :] = gout[:half_w, :]
+    gram_ref[half_w:half_w + half_w // 2, half_w:] = gout[half_w:, :half_w]
+    gram_ref[half_w + half_w // 2:, half_w:] = gout[half_w:, half_w:]
+    gram_ref[half_w:, :half_w] = jnp.zeros((half_w, half_w), F32)
 
 
 def eliminate(a):
@@ -215,20 +224,34 @@
     sub = lax.broadcasted_iota(jnp.int32, (8, n), 0)
     left = [a[8 * g:8 * g + 8, :] for g in range(groups)]
     right = [jnp.where(lane == sub + 8 * g, F32(1.0), F32(0.0)) for g in range(groups)]
-    for j in range(n):
-        g0, s = j // 8, j % 8
-        row = left[g0][s:s + 1, :]
-        inv = F32(1.0) / row[:, j:j + 1]
-        row_l = row * inv
-        row_r = right[g0][s:s + 1, :] * inv
+
+    def across(x, j):
+        return jnp.broadcast_to(x[:, j:j + 1], (8, n))
+
+    def down(x, s):
+        return jnp.broadcast_to(x[s:s + 1, :], (8, n))
+
+    for p in range(0, n, 2):
+        g0, s = p // 8, p % 8
+        cu, cv = across(left[g0], p), across(left[g0], p + 1)
+        a00, a10, a11 = down(cu, s), down(cu, s + 1), down(cv, s + 1)
+        inv_a = F32(1.0) / a00
+        inv_det = F32(1.0) / (a00 * a11 - a10 * a10)
+        m = a10 * inv_a
+        f = a00 * inv_det
+        u, v = down(left[g0], s), down(left[g0], s + 1)
+        ur, vr = down(right[g0], s), down(right[g0], s + 1)
+        ul, url = u * inv_a, ur * inv_a
+        vl, vrl = (v - m * u) * f, (vr - m * ur) * f
         for g in range(g0, groups):
-            if g == g0 and s == 7:
-                continue
-            col = jnp.broadcast_to(left[g][:, j:j + 1], (8, n))
+            if g > g0:
+                cu, cv = across(left[g], p), across(left[g], p + 1)
+            c0, c1 = cu, cv - cu * m
             if g == g0:
-                col = jnp.where(sub > s, col, F32(0.0))
-            left[g] = left[g] - col * row_l
-            right[g] = right[g] - col * row_r
+                c0 = jnp.where(sub > s, c0, F32(0.0))
+                c1 = jnp.where(sub > s + 1, c1, F32(0.0))
+            left[g] = left[g] - c0 * ul - c1 * vl
+            right[g] = right[g] - c0 * url - c1 * vrl
     ups, invs = [], []
     for g in range(groups):
         diag = jnp.sum(jnp.where(lane == sub + 8 * g, left[g], F32(0.0)), axis=1, keepdims=True)
@@ -238,8 +261,15 @@
     return jnp.concatenate(ups, axis=0), jnp.concatenate(invs, axis=0)
 
 
-def factor_kernel(gram_ref, y_ref, r_ref, q_ref, inv_ref):
-    width = gram_ref.shape[0]
+def factor_kernel(gram_in, y_ref, y_out, r_ref, q_ref, inv_ref, gram_ref, y_sem):
+    y_copy = pltpu.make_async_copy(y_ref, y_out, y_sem)
+    y_copy.start()
+    width = gram_in.shape[0]
+    on = lax.broadcasted_iota(jnp.int32, (width, width), 0) == lax.broadcasted_iota(jnp.int32, (width, width), 1)
+    kept = jnp.where(on, gram_in[...], F32(0.0))
+    d_row = jnp.sqrt(jnp.sum(kept, axis=0, keepdims=True))
+    d_col = jnp.sqrt(jnp.sum(kept, axis=1, keepdims=True))
+    gram_ref[...] = gram_in[...] * (F32(1.0) / d_col) * (F32(1.0) / d_row)
     nb = min(128, width)
     blocks = width // nb
 
@@ -268,7 +298,9 @@
             for m in range(j, k):
                 acc = acc + dot(blk(r_ref, m, k), blk(inv_ref, m, j), ((0,), (0,)))
             inv_ref[k * nb:(k + 1) * nb, j * nb:(j + 1) * nb] = -dot(inv, acc, ((1,), (0,)))
-    q_ref[...] = dot(y_ref[...], inv_ref[...], ((1,), (1,)))
+    r_ref[...] = r_ref[...] * d_row
+    q_ref[...] = dot(y_ref[...] * (F32(1.0) / d_row), inv_ref[...], ((1,), (1,)))
+    y_copy.wait()
 
 
 def per_device(n_snp, n_samp, genotypes, basis_cols):
@@ -278,6 +310,7 @@
     chunks = 3
     own = snps // n_samp
     bits = log2(n_snp)
+    packed = width - width // 4
     vmem = pl.BlockSpec(memory_space=pltpu.VMEM)
     dma = pltpu.SemaphoreType.DMA
     y, gram = pl.pallas_call(
@@ -301,10 +334,10 @@
             pltpu.VMEM((n_samp, 8, width), F32),
             pltpu.VMEM((n_samp, own, width), jnp.int16),
             pltpu.VMEM((n_samp, 8, width), F32),
-            pltpu.VMEM((width, width), F32),
-            pltpu.VMEM((width, width), F32),
-            pltpu.VMEM((n_samp, width // n_snp, width), F32),
-            pltpu.VMEM((width, width), F32),
+            pltpu.VMEM((packed, width), F32),
+            pltpu.VMEM((packed, width), F32),
+            pltpu.VMEM((n_samp, packed // n_snp, width), F32),
+            pltpu.VMEM((packed, width), F32),
             dma((chunks, bits)), dma((chunks, bits)), dma((chunks, bits)), dma((chunks, bits)),
             dma((n_snp,)), dma((n_snp,)), dma((n_samp,)), dma((n_samp,)),
             dma((n_samp,)), dma((n_samp,)), dma((n_samp,)), dma((n_samp,)),
@@ -312,15 +345,20 @@
         ],
         compiler_params=pltpu.CompilerParams(collective_id=0, has_side_effects=True),
     )(genotypes, basis_cols)
-    r_factor, q_next = pl.pallas_call(
+    y, r_factor, q_next = pl.pallas_call(
         factor_kernel,
         out_shape=(
+            jax.ShapeDtypeStruct((own, width), F32),
             jax.ShapeDtypeStruct((width, width), F32),
             jax.ShapeDtypeStruct((own, width), F32),
         ),
         in_specs=[vmem, vmem],
-        out_specs=(vmem, vmem),
-        scratch_shapes=[pltpu.VMEM((width, width), F32)],
+        out_specs=(pl.BlockSpec(memory_space=pl.ANY), vmem, vmem),
+        scratch_shapes=[
+            pltpu.VMEM((width, width), F32),
+            pltpu.VMEM((width, width), F32),
+            pltpu.SemaphoreType.DMA,
+        ],
     )(gram, y)
     layout = (1, 1, own, width)
     return (y.reshape(layout), r_factor, q_next.reshape(layout))

time: 94.7 us -> 88.7 us (0.937)
  Pallas kernels: 92 us -> 87.8 us
  local copies, waits for them, and re-layouts: 1.87 us -> 0 us
    pallas_call x1, Pallas kernels: 24.8 us -> 21.6 us  [per_device(): pl.pallas_call(factor_kernel, out_shape=(jax.ShapeDtypeStruct((own, width...]
    unnamed x1 -> x0, local copies, waits for them, and re-layouts: 1.87 us -> none
    pallas_call x1, Pallas kernels: 67.2 us -> 66.2 us  [per_device(): pl.pallas_call(functools.partial(main_kernel, n_snp, n_samp, chunks), out...]
where the time goes in v2:
time: 88.7 us; the launch traced here: 88.6 us
  Pallas kernels  87.8 us (99%)
    pallas_call x1, Pallas kernels, per_device(): pl.pallas_call(functools.partial(main_kernel, n_snp, n_samp, chunks), out...  66.2 us
    pallas_call x1, Pallas kernels, per_device(): pl.pallas_call(factor_kernel, out_shape=(jax.ShapeDtypeStruct((own, width...  21.6 us

profile of v2, /device:TPU:0, one launch (start us, length us, event | category | flops | bytes accessed | tf_op | source)
XLA Modules:
  0.0 88.6 jit_solution(8833996839177407800)
XLA Ops:
  0.6 66.2 %shard_map.49 = (f32[512,256]{1,0:T(8,128)}, f32[256,256]{1,0:T(8,128)}) custom-call(s32[256,2048]{1,0:T(8,128)} %g_ref.1, bf16[2048,256]{1,0:T(8,128)(2,1)} %b_ref.1), custom_call_target="tpu_custom_call" | custom-call | tf_op jit(solution)/shard_map/pallas_call | solution.py:316
  66.8 21.6 %shard_map.50 = (f32[512,256]{1,0:T(8,128)}, f32[256,256]{1,0:T(8,128)}, f32[512,256]{1,0:T(8,128)}) custom-call(f32[256,256]{1,0:T(8,128)} %get-tuple-element.8.gram_in, f32[512,256]{1,0:T(8,128)} %get-tuple-element.9.y_ref), custom_call_target="tpu_custom_call" | custom-call | tf_op jit(solution)/shard_map/pallas_call | solution.py:348

commit v3 on v2

--- a/solution.py
+++ b/solution.py
@@ -37,6 +37,7 @@
     yq, ysc, yq_rx, ysc_rx, gwork, g_rx, gs_rx, gout,
     rs_s, rs_r, ag_s, ag_r, cs_s, cs_r, ct_s, ct_r, yq_s, yq_r, ysc_s, ysc_r,
     gr_s, gr_r, gs_s, gs_r, ga_s, ga_r,
+    coded, coded_rx, meta, meta_rx, mt_s, mt_r,
 ):
     snp, samp = lax.axis_index("snp"), lax.axis_index("samp")
     bits = log2(n_snp)
@@ -73,6 +74,25 @@
             part.at[rows_at(c, send, half)],
             rs_rx.at[pl.ds(c * crow + crow - 2 * half, half)],
             rs_s.at[c, b], rs_r.at[c, b], "snp", partner(b),
+        )
+
+    def code(c, b):
+        keep, send, half = steps[b]
+        block = part[rows_at(c, send, half), :]
+        mean = jnp.sum(block, axis=0, keepdims=True) * F32(1.0 / half)
+        block = block - mean
+        top = jnp.maximum(jnp.max(jnp.abs(block), axis=0, keepdims=True), F32(1e-30))
+        off = c * crow + crow - 2 * half
+        coded[pl.ds(off, half), :] = jnp.round(block * (F32(LEVELS) / top)).astype(jnp.int32).astype(jnp.int16)
+        meta[c, b, 0:8, :] = jnp.broadcast_to(top * F32(1.0 / LEVELS), (8, width))
+        meta[c, b, 8:16, :] = jnp.broadcast_to(mean, (8, width))
+
+    def coded_copies(c, b):
+        half = steps[b][2]
+        seg = pl.ds(c * crow + crow - 2 * half, half)
+        return (
+            copy(coded.at[seg], coded_rx.at[seg], rs_s.at[c, b], rs_r.at[c, b], "snp", partner(b)),
+            copy(meta.at[c, b], meta_rx.at[c, b], mt_s.at[c, b], mt_r.at[c, b], "snp", partner(b)),
         )
 
     def ag_copy(c, b):
@@ -105,12 +125,21 @@
     def reduce_step(b, center=None):
         for c in range(chunks):
             keep, send, half = steps[b]
-            rs_copy(c, b).wait()
             seg = rows_at(c, keep, half)
-            total = part[seg, :] + rs_rx[pl.ds(c * crow + crow - 2 * half, half), :]
+            arrived = pl.ds(c * crow + crow - 2 * half, half)
+            if b == 0:
+                rs_copy(c, b).wait()
+                total = part[seg, :] + rs_rx[arrived, :]
+            else:
+                for cp in coded_copies(c, b):
+                    cp.wait()
+                other = coded_rx[arrived, :].astype(jnp.int32).astype(F32) * meta_rx[c, b, 0:1, :]
+                total = part[seg, :] + (other + meta_rx[c, b, 8:9, :])
             if b + 1 < bits:
                 part[seg, :] = total
-                rs_copy(c, b + 1).start()
+                code(c, b + 1)
+                for cp in coded_copies(c, b + 1):
+                    cp.start()
             else:
                 scores[seg, :] = (total - center).astype(BF16)
                 ag_copy(c, b).start()
@@ -231,27 +260,42 @@
     def down(x, s):
         return jnp.broadcast_to(x[s:s + 1, :], (8, n))
 
-    for p in range(0, n, 2):
-        g0, s = p // 8, p % 8
-        cu, cv = across(left[g0], p), across(left[g0], p + 1)
-        a00, a10, a11 = down(cu, s), down(cu, s + 1), down(cv, s + 1)
-        inv_a = F32(1.0) / a00
-        inv_det = F32(1.0) / (a00 * a11 - a10 * a10)
-        m = a10 * inv_a
-        f = a00 * inv_det
-        u, v = down(left[g0], s), down(left[g0], s + 1)
-        ur, vr = down(right[g0], s), down(right[g0], s + 1)
-        ul, url = u * inv_a, ur * inv_a
-        vl, vrl = (v - m * u) * f, (vr - m * ur) * f
-        for g in range(g0, groups):
-            if g > g0:
-                cu, cv = across(left[g], p), across(left[g], p + 1)
-            c0, c1 = cu, cv - cu * m
-            if g == g0:
-                c0 = jnp.where(sub > s, c0, F32(0.0))
-                c1 = jnp.where(sub > s + 1, c1, F32(0.0))
-            left[g] = left[g] - c0 * ul - c1 * vl
-            right[g] = right[g] - c0 * url - c1 * vrl
+    for g0 in range(groups):
+        jl, jr = left[g0], right[g0]
+        cols = [across(jl, 8 * g0 + i) for i in range(8)]
+        up_l, up_r = jl, jr
+        for s in range(0, 8, 2):
+            c0, c1 = cols[s], cols[s + 1]
+            a00, a10, a11 = down(c0, s), down(c0, s + 1), down(c1, s + 1)
+            inv_a = F32(1.0) / a00
+            inv_det = F32(1.0) / (a00 * a11 - a10 * a10)
+            m = a10 * inv_a
+            f = a00 * inv_det
+
+            def step(x):
+                u, v = down(x, s), down(x, s + 1)
+                v = v - m * u
+                w1 = v * f
+                w0 = u * inv_a - m * w1
+                x = x - c0 * w0 - c1 * w1
+                return u, v, jnp.where(sub == s, w0, jnp.where(sub == s + 1, w1, x))
+
+            for i in range(s + 2, 8):
+                cols[i] = step(cols[i])[2]
+            u, v, jl = step(jl)
+            up_l = jnp.where(sub == s, u, jnp.where(sub == s + 1, v, up_l))
+            u, v, jr = step(jr)
+            up_r = jnp.where(sub == s, u, jnp.where(sub == s + 1, v, up_r))
+        left[g0], right[g0] = up_l, up_r
+        rows_l = [down(jl, i) for i in range(8)]
+        rows_r = [down(jr, i) for i in range(8)]
+        for g in range(g0 + 1, groups):
+            xl, xr = left[g], right[g]
+            for i in range(8):
+                col = across(left[g], 8 * g0 + i)
+                xl = xl - col * rows_l[i]
+                xr = xr - col * rows_r[i]
+            left[g], right[g] = xl, xr
     ups, invs = [], []
     for g in range(groups):
         diag = jnp.sum(jnp.where(lane == sub + 8 * g, left[g], F32(0.0)), axis=1, keepdims=True)
@@ -342,6 +386,11 @@
             dma((n_snp,)), dma((n_snp,)), dma((n_samp,)), dma((n_samp,)),
             dma((n_samp,)), dma((n_samp,)), dma((n_samp,)), dma((n_samp,)),
             dma((bits,)), dma((bits,)), dma((n_samp,)), dma((n_samp,)), dma((bits,)), dma((bits,)),
+            pltpu.VMEM((rows, width), jnp.int16),
+            pltpu.VMEM((rows, width), jnp.int16),
+            pltpu.VMEM((chunks, bits, 16, width), F32),
+            pltpu.VMEM((chunks, bits, 16, width), F32),
+            dma((chunks, bits)), dma((chunks, bits)),
         ],
         compiler_params=pltpu.CompilerParams(collective_id=0, has_side_effects=True),
     )(genotypes, basis_cols)

time: 88.7 us -> 77.4 us (0.87)
  Pallas kernels: 87.8 us -> 76.4 us
    pallas_call x1, Pallas kernels: 21.6 us -> 13.2 us  [per_device(): pl.pallas_call(factor_kernel, out_shape=(jax.ShapeDtypeStruct((own, width...]
    pallas_call x1, Pallas kernels: 66.2 us -> 63.3 us  [per_device(): pl.pallas_call(functools.partial(main_kernel, n_snp, n_samp, chunks), out...]
where the time goes in v3:
time: 77.4 us; the launch traced here: 77.2 us
  Pallas kernels  76.4 us (99%)
  between operations  0.8 us (1%)
    pallas_call x1, Pallas kernels, per_device(): pl.pallas_call(functools.partial(main_kernel, n_snp, n_samp, chunks), out...  63.3 us
    pallas_call x1, Pallas kernels, per_device(): pl.pallas_call(factor_kernel, out_shape=(jax.ShapeDtypeStruct((own, width...  13.2 us

profile of v3, /device:TPU:0, one launch (start us, length us, event | category | flops | bytes accessed | tf_op | source)
XLA Modules:
  0.0 77.2 jit_solution(6253046184797564253)
XLA Ops:
  0.6 63.3 %shard_map.49 = (f32[512,256]{1,0:T(8,128)}, f32[256,256]{1,0:T(8,128)}) custom-call(s32[256,2048]{1,0:T(8,128)} %g_ref.1, bf16[2048,256]{1,0:T(8,128)(2,1)} %b_ref.1), custom_call_target="tpu_custom_call" | custom-call | tf_op jit(solution)/shard_map/pallas_call | solution.py:360
  63.9 13.2 %shard_map.50 = (f32[512,256]{1,0:T(8,128)}, f32[256,256]{1,0:T(8,128)}, f32[512,256]{1,0:T(8,128)}) custom-call(f32[256,256]{1,0:T(8,128)} %get-tuple-element.8.gram_in, f32[512,256]{1,0:T(8,128)} %get-tuple-element.9.y_ref), custom_call_target="tpu_custom_call" | custom-call | tf_op jit(solution)/shard_map/pallas_call | solution.py:397
